TPU v7x, 768 devices: a whole 4x8x12 slice. The times are simulated.
768 devices in a mesh: tm: 96 (over z_lo, y, core), space: 8 (over z_hi, x).
Axes of the slice: x: 4, y: 8, z: 12 (z_hi: 2, z_lo: 6; z = z_hi * 6 + z_lo), core: 2. Of those that a mesh axis runs over, the one named last changes fastest.
Arguments:
- eigvecs: bfloat16 [2, 3, 96, 4096, 256], P(None, None, 'tm', 'space'), may hold values from -0.09375 to 0.09375
- propagator: bfloat16 [2, 3, 96, 4096, 128], P(None, None, 'tm', 'space'), may hold values from -6 to 6
- elementals: bfloat16 [96, 8, 2, 256, 256], P('tm'), may hold values from -0.0017089844 to 0.0017089844
- sink_times: int32 [96, 16], P('tm'), may hold values from 0 to 95, as said below
- momenta: int32 [96, 16], P('tm'), may hold values from 0 to 7
Outputs:
- traces: float32 [2, 96, 16], P(None, 'tm')
Inputs may be any that keep to these rules, and one draw needn't show every extreme that they name: (sink_times[t, k] - t) modulo 96 lies in 0 to 49 or equals 95; item 0 of every slice t has sink time (t + 48) modulo 96, item 1 has (t - 1) modulo 96.
All inputs are finite; a program needn't handle non-finite values.
Results may differ from a plain program's by a relative error of at most 0.0049.
Values may be sent and summed in bfloat16 or wider, within the bound.
A program may use at most 32 MiB of HBM per device.

v0:
```python
import jax
import jax.numpy as jnp
from jax import lax
from jax.sharding import PartitionSpec as P


def on_device(eigvecs, propagator, elementals, sink_times, momenta):
    vec_count = eigvecs.shape[-1]
    column_count = propagator.shape[-1]
    momentum_count = elementals.shape[1]
    groups = lax.axis_size("space")
    vecs_flat = eigvecs.reshape(2, -1, vec_count)
    columns_both = jnp.concatenate([vecs_flat[0], vecs_flat[1]], axis=0)
    columns_swap = jnp.concatenate([-vecs_flat[1], vecs_flat[0]], axis=0)
    vec_both = jnp.stack([columns_both, columns_swap], axis=1)
    prop_cat = propagator.reshape(-1, column_count)
    moments = elementals[0]
    shard_size = vec_count // groups
    own_block = lax.psum_scatter(
        jnp.einsum("kqa,ks->aqs", vec_both, prop_cat, preferred_element_type=jnp.float32),
        "space",
        scatter_dimension=0,
        tiled=True,
    ).astype(jnp.bfloat16)
    gathered = lax.all_gather(own_block, "space", axis=0, tiled=True)
    own_rows = lax.dynamic_slice_in_dim(
        moments, lax.axis_index("space") * shard_size, shard_size, 2
    )
    expand = jnp.einsum("prab,bqs->praqs", own_rows, gathered, preferred_element_type=jnp.float32)
    real_part = expand[:, 0, :, 0] - expand[:, 1, :, 1]
    imag_part = expand[:, 0, :, 1] + expand[:, 1, :, 0]
    mixed_terms = jnp.stack([real_part, imag_part], axis=2).astype(jnp.bfloat16)
    swapped = jnp.stack([mixed_terms[:, :, 1], -mixed_terms[:, :, 0]], axis=2)
    weights = jnp.stack([mixed_terms, swapped], axis=1).reshape(2 * momentum_count, -1)
    time_slots = lax.axis_size("tm")
    pick_mom = (momenta[0][:, None] == jnp.arange(momentum_count, dtype=jnp.int32)[None, :]).astype(
        jnp.float32
    )
    blocks = lax.all_gather(own_block[None], "tm", axis=0, tiled=True)
    flattened = blocks.reshape(blocks.shape[0], -1)
    values = lax.dot_general(
        weights, flattened, (((1,), (1,)), ((), ())), preferred_element_type=jnp.float32
    )
    tables = values
    slot_index = sink_times[0]
    tables = tables.reshape(momentum_count, 2, time_slots)
    pick_time = (slot_index[:, None] == jnp.arange(time_slots, dtype=jnp.int32)[None, :]).astype(
        jnp.float32
    )
    spread = jnp.einsum("kp,pot->okt", pick_mom, tables, precision=lax.Precision.HIGHEST)
    picked = jnp.sum(spread * pick_time[None], axis=2)
    summed = lax.psum(picked, "space")
    return summed[:, None, :]


def solution(mesh):
    return jax.shard_map(
        on_device,
        mesh=mesh,
        in_specs=(
            P(None, None, "tm", "space", None),
            P(None, None, "tm", "space", None),
            P("tm", None, None, None, None),
            P("tm", None),
            P("tm", None),
        ),
        out_specs=P(None, "tm", None),
        check_vma=False,
    )
```

profile of v0, /device:TPU:1, one launch (start us, length us, event | category | flops | bytes accessed | tf_op | source)
XLA Modules:
  0.0 339.5 jit_solution(5826366558176417054)
XLA Ops:
  6.5 0.0 copy-start
  6.5 0.0 reduce-scatter.2.cloned.1.call-start
  6.5 2.8 fusion.29
  9.3 1.4 copy.15
  10.7 1.0 neg.7
  11.8 2.3 copy.14
  14.1 0.0 copy-start.2
  14.1 2.1 maximum_bitcast_fusion
  16.1 0.0 copy-done.2
  16.2 0.0 copy-start.1
  16.2 1.7 fusion.6
  17.8 0.0 reduce-scatter.2.cloned.1.call-update
  17.9 0.0 all-gather.3.cloned.1.call-start
  17.9 108.4 %reduce-scatter.2.cloned.1.call-done = f32[32,2,128]{2,0,1:T(8,128)} async-done(((f32[256,2,128]{2,0,1:T(8,128)}), f32[32,2,128]{2,0,1:T(8,128)}) %reduce-scatter.2.cloned.1.call-update) | async-done | bytes 32784 | tf_op jit(solution)/shard_map/reduce_scatter | solution.py:19
  126.3 1.4 convert_element_type.19
  127.7 0.0 all-gather.3.cloned.1.call-update
  127.7 0.0 copy-done.1
  127.7 0.1 fusion.22
  127.8 47.3 %all_gather.6 = bf16[256,2,128]{2,0,1:T(8,128)(2,1)S(1)} all-gather(bf16[32,2,128]{2,0,1:T(8,128)(2,1)} %convert_element_type.19), channel_id=1, replica_groups=mesh['tm'=96,'space'=8] {'space'}, dimensions={0}, use_global_device_ids=true | all-gather | bytes 147456 | tf_op jit(solution)/shard_map/all_gather | solution.py:25
  175.1 0.0 copy-done
  175.1 0.2 fusion.14
  175.4 0.0 copy-start.3
  175.5 121.1 %all-gather.3.cloned.1.call-done = bf16[3072,2,128]{2,0,1:T(8,128)(2,1)} async-done(((bf16[32,2,128]{2,0,1:T(8,128)(2,1)}), bf16[3072,2,128]{2,0,1:T(8,128)(2,1)}) %all-gather.3.cloned.1.call-update) | async-done | bytes 1572880 | tf_op jit(solution)/shard_map/all_gather | solution.py:39
  296.6 2.0 fusion.11
  298.6 0.0 copy-done.3
  298.6 0.3 fusion.10
  298.9 33.8 %psum.7 = f32[2,1,16]{2,0,1:T(2,128)} all-reduce(f32[2,1,16]{2,0,1:T(2,128)S(1)} %bitcast.69), channel_id=1, replica_groups=mesh['tm'=96,'space'=8] {'space'}, use_global_device_ids=true, to_apply=%region_2.0 | all-reduce | flops 32 | bytes 256 | tf_op jit(solution)/shard_map/psum | solution.py:52
  (5 shorter events, 0.1 us)
Async XLA Ops:
  6.5 168.6 %copy-start = (bf16[1,8,2,256,256]{4,3,2,1,0:T(8,128)(2,1)S(1)}, bf16[1,8,2,256,256]{4,3,2,1,0:T(8,128)(2,1)}, u32[]{:S(2)}) copy-start(bf16[1,8,2,256,256]{4,3,2,1,0:T(8,128)(2,1)} %param.7) | copy-start | bytes 6291460
  6.5 119.8 %reduce-scatter.2.cloned.1.call-start = ((), (), s32[]{:S(2)}) async-start(), calls=%async_computation.1 | async-start | bytes 294912 | tf_op jit(solution)/shard_map/reduce_scatter | solution.py:19
  14.1 2.1 copy-start.2
  16.2 111.5 %copy-start.1 = (s32[1,16]{1,0:T(1,128)S(1)}, s32[1,16]{1,0:T(1,128)}, u32[]{:S(2)}) copy-start(s32[1,16]{1,0:T(1,128)} %param.8) | copy-start | bytes 196
  17.9 278.7 %all-gather.3.cloned.1.call-start = ((), (), s32[]{:S(2)}) async-start(), calls=%async_computation.2 | async-start | bytes 1589248 | tf_op jit(solution)/shard_map/all_gather | solution.py:39
  175.4 123.2 %copy-start.3 = (s32[1,16]{1,0:T(1,128)S(1)}, s32[1,16]{1,0:T(1,128)}, u32[]{:S(2)}) copy-start(s32[1,16]{1,0:T(1,128)} %param.9) | copy-start | bytes 196
Sparse Core Ops, SparseCore 0:
  18.0 108.2 reduce-scatter.1
  128.7 167.8 all-gather.2
where the time goes:
time: 343 us; the launch traced here: 339 us
  waiting for transfers between devices  230 us (67%)
  blocking collectives  81.1 us (24%)
  between operations  13.5 us (4%)
  local copies, waits for them, and re-layouts  6.51 us (2%)
  other arithmetic  4.65 us (1%)
  matrix products  4.19 us (1%)
    all_gather x1, waiting for transfers between devices, on_device(): blocks = lax.all_gather(own_block[None], 'tm', axis=0, tiled=True)  121 us
    reduce_scatter x1, waiting for transfers between devices, on_device(): lax.psum_scatter(jnp.einsum('kqa,ks->aqs', vec_both, prop_cat, preferred_...  108 us
    all_gather x1, blocking collectives, on_device(): gathered = lax.all_gather(own_block, 'space', axis=0, tiled=True)  47.3 us
    psum x1, blocking collectives, on_device(): summed = lax.psum(picked, 'space')  33.8 us
  transfers between devices with their start and end apart: 2, of which 2 were waited for; matrix products, arithmetic and copies ran while one was open for 0% of the time, Pallas kernels for 0%

commit v1 on v0

v1 whole, which is shorter than its diff:
```python
import functools

import jax
import jax.numpy as jnp
from jax import lax
from jax.experimental import pallas as pl
from jax.experimental.pallas import tpu as pltpu
from jax.sharding import PartitionSpec as P

X, Y, ZL, CORES = 4, 8, 6, 2
ZR = 2 * ZL
OFFSETS = (6, 7, 1, 8, 2, 9, 3)
F32 = jnp.float32
BF16 = jnp.bfloat16


def kernel(
    vec_hbm, prop_hbm, elem_hbm, sink_hbm, mom_hbm, out_ref,
    vec, prop, elem, xsend, xrecv, zsend, zrecv, gath, mix, sink, mom, rows, ranks,
    load_sem, elem_sem, item_sem, item_send, item_recv,
    xs_sem, xr_sem, zs_sem, zr_sem, ys_sem, yr_sem, mix_sem, fs_sem, fr_sem,
):
    tm, space = lax.axis_index("tm"), lax.axis_index("space")
    core, chip = lax.rem(tm, 2), lax.div(tm, 2)
    y, c = lax.rem(chip, Y), lax.div(chip, Y)
    h, x = lax.div(space, X), lax.rem(space, X)
    ring = h * ZL + c
    columns = prop.shape[-1]
    wide = columns // X
    narrow = wide // 2

    def device(xx, yy, zz, kk):
        hh, cc = lax.div(zz, ZL), lax.rem(zz, ZL)
        return {"tm": (cc * Y + yy) * 2 + kk, "space": hh * X + xx}

    def send(src, dst, ssem, rsem, where):
        return pltpu.make_async_remote_copy(
            src_ref=src, dst_ref=dst, send_sem=ssem, recv_sem=rsem,
            device_id=where, device_id_type=pl.DeviceIdType.MESH,
        )

    far = lax.rem(ring + ZL, ZR)
    special = jnp.logical_or(
        jnp.logical_and(y == 0, core == 0), jnp.logical_and(y == Y - 1, core == 1)
    )
    final = [
        (dx, dz, dk) for dz in range(2) for dx in range(X) for dk in range(2) if dx or dz or dk
    ]

    def final_device(dx, dz, dk):
        return device(
            lax.rem(x + dx, X), y, far if dz else ring, (1 - core) if dk else core
        )

    loads = []
    for q in range(2):
        for col in range(3):
            a = pltpu.make_async_copy(vec_hbm.at[q, col, 0], vec.at[q, col], load_sem.at[0, q, col])
            b = pltpu.make_async_copy(prop_hbm.at[q, col, 0], prop.at[q, col], load_sem.at[1, q, col])
            a.start()
            b.start()
            loads.append((a, b))
    elem_load = pltpu.make_async_copy(elem_hbm.at[0], elem, elem_sem)
    elem_load.start()
    own_items = [
        pltpu.make_async_copy(sink_hbm, sink.at[pl.ds(core, 1)], item_sem.at[0]),
        pltpu.make_async_copy(mom_hbm, mom.at[pl.ds(core, 1)], item_sem.at[1]),
    ]
    for copy in own_items:
        copy.start()

    barrier = pltpu.get_barrier_semaphore()
    partners = [final_device(*d) for d in final]
    partners += [device(x, lax.rem(y + r, Y), ring, core) for r in range(1, Y)]
    partners += [device(x, y, lax.rem(ring + r, ZR), core) for r in range(1, ZR) if r != ZL]
    for where in partners:
        pl.semaphore_signal(barrier, inc=1, device_id=where, device_id_type=pl.DeviceIdType.MESH)

    dims = (((0,), (0,)), ((), ()))
    real = imag = None
    for col in range(3):
        for q in range(2):
            for copy in loads[q * 3 + col]:
                copy.wait()
        vr, vi = vec[0, col], vec[1, col]
        pr, pi = prop[0, col], prop[1, col]
        dot = functools.partial(lax.dot_general, dimension_numbers=dims, preferred_element_type=F32)
        re = dot(pr, vr) + dot(pi, vi)
        im = dot(pi, vr) - dot(pr, vi)
        real = re if real is None else real + re
        imag = im if imag is None else imag + im
    for xx in range(X):
        xsend[xx, 0] = real[xx * wide:(xx + 1) * wide]
        xsend[xx, 1] = imag[xx * wide:(xx + 1) * wide]

    pl.semaphore_wait(barrier, len(partners))

    xcopies = []
    for d in (2, 1, 3):
        xx = lax.rem(x + d, X)
        copy = send(
            xsend.at[xx], xrecv.at[x], xs_sem.at[d], xr_sem.at[x], device(xx, y, ring, core)
        )
        copy.start()
        xcopies.append(copy)
    other = device(x, y, ring, 1 - core)
    for copy in own_items:
        copy.wait()
    items = [
        send(sink_hbm, sink.at[pl.ds(core, 1)], item_send.at[0], item_recv.at[0], other),
        send(mom_hbm, mom.at[pl.ds(core, 1)], item_send.at[1], item_recv.at[1], other),
    ]
    for copy in items:
        copy.start()
    total = xsend[x]
    for d in (1, 3, 2):
        xx = lax.rem(x + d, X)
        pltpu.make_async_copy(xrecv.at[xx], xrecv.at[xx], xr_sem.at[xx]).wait()
        total = total + xrecv[xx]
    for hh in range(2):
        zsend[hh] = total[:, hh * narrow:(hh + 1) * narrow]

    def zcopy(off, slot):
        to = lax.rem(ring + ZR - off, ZR)
        return send(
            zsend.at[lax.div(to, ZL)], zrecv.at[slot], zs_sem.at[slot], zr_sem.at[slot],
            device(x, y, to, core),
        )

    zcopies = [zcopy(off, slot) for slot, off in enumerate(OFFSETS)]
    for copy in zcopies:
        copy.start()

    @pl.when(special)
    def _():
        zcopy(4 + core, 7).start()
        zcopy(10 + core, 8).start()

    def arrived(slot):
        pltpu.make_async_copy(zrecv.at[slot], zrecv.at[slot], zr_sem.at[slot]).wait()
        return zrecv[slot]

    def ysend(src, dst, n, kind, r):
        yy = lax.rem(y + r, Y)
        return send(
            src, dst, ys_sem.at[kind, r], yr_sem.at[kind, y], device(x, yy, ring, core)
        )

    order = (4, 3, 5, 2, 6, 1, 7)
    ycopies = []
    gath[y, 0] = (arrived(2) + arrived(1)).astype(BF16)
    gath[y, 1] = (arrived(4) + arrived(3)).astype(BF16)
    for r in order:
        ycopies.append(ysend(gath.at[y, pl.ds(0, 2)], gath.at[y, pl.ds(0, 2)], 2, 0, r))
        ycopies[-1].start()
    gath[y, 3] = (arrived(6) + arrived(5)).astype(BF16)
    own = (zsend[h] + arrived(0)).astype(BF16)
    gath[y, 2] = own
    for r in order:
        yy = lax.rem(y + r, Y)
        slot = jnp.where(y >= yy, 2, 3)
        ycopies.append(ysend(gath.at[y, slot], gath.at[y, 2], 1, 1, r))
        ycopies[-1].start()

    @pl.when(special)
    def _():
        gath[y, 4] = (arrived(7) + arrived(8)).astype(BF16)

    slot = jnp.where(special, 4, jnp.where(core == 0, 3, 2))
    step = jnp.where(core == 0, Y - 1, 1)
    extra = send(
        gath.at[y, slot], gath.at[y, 3], ys_sem.at[2, 0], yr_sem.at[2, 0],
        device(x, lax.rem(y + step, Y), ring, core),
    )
    extra.start()

    elem_load.wait()
    stacked = jnp.concatenate([own[0], own[1]], axis=0)
    nt = (((1,), (1,)), ((), ()))
    for p in range(elem.shape[0]):
        by_real = lax.dot_general(stacked, elem[p, 0], nt, preferred_element_type=F32)
        by_imag = lax.dot_general(stacked, elem[p, 1], nt, preferred_element_type=F32)
        mix[core, p, 0] = (by_real[:narrow] - by_imag[narrow:]).astype(BF16)
        mix[core, p, 1] = (by_real[narrow:] + by_imag[:narrow]).astype(BF16)
    mix_copy = send(mix.at[core], mix.at[core], mix_sem.at[0], mix_sem.at[1], other)
    mix_copy.start()

    for copy in items:
        copy.wait_recv()
    mix_copy.wait_recv()
    for r in range(1, Y):
        yy = lax.rem(y + r, Y)
        both = gath.at[yy, pl.ds(0, 2)]
        pltpu.make_async_copy(both, both, yr_sem.at[0, yy]).wait()
        pltpu.make_async_copy(gath.at[yy, 2], gath.at[yy, 2], yr_sem.at[1, yy]).wait()
    extra.wait_recv()

    ranks[...] = jnp.zeros_like(ranks)
    lanes = ranks.shape[-1]
    count = sink.shape[-1]
    for kt in range(2):
        @pl.loop(0, count)
        def _(k):
            rel = sink[kt, k] + (ZL - c) * (2 * Y)
            rel = jnp.where(rel >= ZL * 2 * Y, rel - ZL * 2 * Y, rel)
            cls = rel // (2 * Y)
            rest = rel - cls * (2 * Y)
            yy = rest // 2
            kk = rest - yy * 2
            third = jnp.where(yy >= y, 0, 3)
            slot = jnp.where(cls == 1, 0, jnp.where(cls == 2, 1, jnp.where(cls == third, 2, 3)))
            g = gath[yy, slot].astype(F32)
            m = mix[kt, mom[kt, k]].astype(F32)
            keep = kk == core
            re = g[0] * m[0] + g[1] * m[1]
            im = g[0] * m[1] - g[1] * m[0]
            for o, v in ((0, re), (1, im)):
                s = v[:, :lanes]
                for part in range(1, v.shape[1] // lanes):
                    s = s + v[:, part * lanes:(part + 1) * lanes]
                s = jnp.where(keep, jnp.sum(s, axis=0, keepdims=True), 0.0)
                ranks[pl.ds((kt * 2 + o) * count + k, 1)] = s

    me = space * 2 + core
    row = lax.dot_general(
        jnp.ones((8, lanes), F32), ranks[...], nt,
        precision=lax.Precision.HIGHEST, preferred_element_type=F32,
    )
    rows[me] = row[:1]
    fcopies = []
    for n, d in enumerate(final):
        copy = send(rows.at[me], rows.at[me], fs_sem.at[n], fr_sem.at[me], final_device(*d))
        copy.start()
        fcopies.append(copy)
    for dx, dz, dk in final:
        src = lax.rem(h + dz, 2) * X + lax.rem(x + dx, X)
        src = src * 2 + ((1 - core) if dk else core)
        pltpu.make_async_copy(rows.at[src], rows.at[src], fr_sem.at[src]).wait()
    acc = rows[0]
    for n in range(1, 4 * X):
        acc = acc + rows[n]
    mine = jnp.where(core == 0, acc[:, :2 * count], acc[:, 2 * count:4 * count])
    out_ref[0:1] = mine[:, :count]
    out_ref[1:2] = mine[:, count:]

    for copy in xcopies + items + zcopies + ycopies + [extra, mix_copy] + fcopies:
        copy.wait_send()
    @pl.when(special)
    def _():
        zcopy(4 + core, 7).wait_send()
        zcopy(10 + core, 8).wait_send()


def on_device(eigvecs, propagator, elementals, sink_times, momenta):
    nvec, cols, sites = eigvecs.shape[-1], propagator.shape[-1], eigvecs.shape[3]
    nmom, items = elementals.shape[1], sink_times.shape[1]
    wide, narrow = cols // X, cols // X // 2
    dma = pltpu.SemaphoreType.DMA
    out = pl.pallas_call(
        kernel,
        out_shape=jax.ShapeDtypeStruct((2, items), F32),
        in_specs=[pl.BlockSpec(memory_space=pl.ANY)] * 5,
        out_specs=pl.BlockSpec(memory_space=pltpu.VMEM),
        scratch_shapes=[
            pltpu.VMEM((2, 3, sites, nvec), BF16),
            pltpu.VMEM((2, 3, sites, cols), BF16),
            pltpu.VMEM((nmom, 2, nvec, nvec), BF16),
            pltpu.VMEM((X, 2, wide, nvec), F32),
            pltpu.VMEM((X, 2, wide, nvec), F32),
            pltpu.VMEM((2, 2, narrow, nvec), F32),
            pltpu.VMEM((9, 2, narrow, nvec), F32),
            pltpu.VMEM((Y, 5, 2, narrow, nvec), BF16),
            pltpu.VMEM((2, nmom, 2, narrow, nvec), BF16),
            pltpu.SMEM((2, items), jnp.int32),
            pltpu.SMEM((2, items), jnp.int32),
            pltpu.VMEM((4 * X, 1, 128), F32),
            pltpu.VMEM((128, 128), F32),
            dma((2, 2, 3)), dma, dma((2,)), dma((2,)), dma((2,)),
            dma((X,)), dma((X,)), dma((9,)), dma((9,)), dma((3, Y)), dma((3, Y)),
            dma((2,)), dma((4 * X,)), dma((4 * X,)),
        ],
        compiler_params=pltpu.CompilerParams(
            collective_id=0, has_side_effects=True, vmem_limit_bytes=32 * 1024 * 1024
        ),
    )(eigvecs, propagator, elementals, sink_times, momenta)
    return out[:, None, :]


def solution(mesh):
    return jax.shard_map(
        on_device,
        mesh=mesh,
        in_specs=(
            P(None, None, "tm", "space", None),
            P(None, None, "tm", "space", None),
            P("tm", None, None, None, None),
            P("tm", None),
            P("tm", None),
        ),
        out_specs=P(None, "tm", None),
        check_vma=False,
    )
```

time: 343 us -> 65.3 us (0.19)
  waiting for transfers between devices: 230 us -> 0 us
  blocking collectives: 81.1 us -> 0 us
  Pallas kernels: 0 us -> 59.1 us
  between operations: 13.5 us -> 0.01 us
  other arithmetic: 4.65 us -> 0 us
  matrix products: 4.19 us -> 0 us
    all_gather x1 -> x0, waiting for transfers between devices: 121 us -> none  [on_device(): blocks = lax.all_gather(own_block[None], 'tm', axis=0, tiled=True)]
    reduce_scatter x1 -> x0, waiting for transfers between devices: 108 us -> none  [on_device(): lax.psum_scatter(jnp.einsum('kqa,ks->aqs', vec_both, prop_cat, preferred_...]
    pallas_call x0 -> x1, Pallas kernels: none -> 59.1 us  [on_device(): pl.pallas_call(kernel, out_shape=jax.ShapeDtypeStruct((2, items), F32), i...]
    all_gather x1 -> x0, blocking collectives: 47.3 us -> none  [on_device(): gathered = lax.all_gather(own_block, 'space', axis=0, tiled=True)]
    psum x1 -> x0, blocking collectives: 33.8 us -> none  [on_device(): summed = lax.psum(picked, 'space')]
    unnamed x8 -> x11, local copies, waits for them, and re-layouts: 0.02 us -> 6 us
    dot_general x4 -> x0, matrix products: 4.19 us -> none  [the longest x1 2.01 us: on_device(): lax.dot_general(weights, flattened, (((1,), (1,)), ((), ())), preferred_e...]
    squeeze x2 -> x0, local copies, waits for them, and re-layouts: 3.71 us -> none  [on_device(): columns_both = jnp.concatenate([vecs_flat[0], vecs_flat[1]], axis=0)]
  transfers between devices with their start and end apart: 2 -> 0, of which waited for: 2 -> 0; matrix products, arithmetic and copies ran while one was open for 0% -> 0% of each run, Pallas kernels for 0% -> 0%
where the time goes in v1:
time: 65.3 us; the launch traced here: 65.1 us
  Pallas kernels  59.1 us (91%)
  local copies, waits for them, and re-layouts  6 us (9%)
    pallas_call x1, Pallas kernels, on_device(): pl.pallas_call(kernel, out_shape=jax.ShapeDtypeStruct((2, items), F32), i...  59.1 us
    unnamed x11, local copies, waits for them, and re-layouts  6 us

profile of v1, /device:TPU:1, one launch (start us, length us, event | category | flops | bytes accessed | tf_op | source)
XLA Modules:
  0.0 65.1 jit_solution(15233215320712392880)
XLA Ops:
  0.0 0.0 copy-start
  0.0 1.6 %copy-done = bf16[1,8,2,256,256]{4,3,2,1,0:T(8,128)(2,1)S(1)} copy-done((bf16[1,8,2,256,256]{4,3,2,1,0:T(8,128)(2,1)S(1)}, bf16[1,8,2,256,256]{4,3,2,1,0:T(8,128)(2,1)}, u32[]{:S(2)}) %copy-start) | copy-done | bytes 2097176
  1.6 0.0 copy-start.1
  1.6 1.4 %copy-done.1 = bf16[2,3,1,512,256]{4,3,2,1,0:T(8,128)(2,1)S(1)} copy-done((bf16[2,3,1,512,256]{4,3,2,1,0:T(8,128)(2,1)S(1)}, bf16[2,3,1,512,256]{4,3,2,1,0:T(8,128)(2,1)}, u32[]{:S(2)}) %copy-start.1) | copy-done | bytes 1572888
  3.0 0.0 copy-start.2
  3.0 1.1 %copy-done.2 = bf16[2,3,1,512,128]{4,3,2,1,0:T(8,128)(2,1)S(1)} copy-done((bf16[2,3,1,512,128]{4,3,2,1,0:T(8,128)(2,1)S(1)}, bf16[2,3,1,512,128]{4,3,2,1,0:T(8,128)(2,1)}, u32[]{:S(2)}) %copy-start.2) | copy-done | bytes 786456
  4.1 0.0 copy-start.3
  4.1 0.7 %copy-done.3 = s32[1,16]{1,0:T(1,128)S(1)} copy-done((s32[1,16]{1,0:T(1,128)S(1)}, s32[1,16]{1,0:T(1,128)}, u32[]{:S(2)}) %copy-start.3) | copy-done | bytes 88
  4.8 0.0 copy-start.4
  4.8 0.7 %copy-done.4 = s32[1,16]{1,0:T(1,128)S(1)} copy-done((s32[1,16]{1,0:T(1,128)S(1)}, s32[1,16]{1,0:T(1,128)}, u32[]{:S(2)}) %copy-start.4) | copy-done | bytes 88
  5.4 59.1 %shard_map.55 = f32[2,16]{1,0:T(2,128)S(1)} custom-call(bf16[2,3,1,512,256]{4,3,2,1,0:T(8,128)(2,1)S(1)} %copy-done.1, bf16[2,3,1,512,128]{4,3,2,1,0:T(8,128)(2,1)S(1)} %copy-done.2, bf16[1,8,2,256,256]{4,3,2,1,0:T(8,128)(2,1)S(1)} %copy-done, s32[1,16]{1,0:T(1,128)S(1)} %copy-done.3, s32[1,16]{1,0:T(1,128)S(1)} %copy-done.4), custom_call_target="tpu_custom_call" | custom-call | tf_op jit(solution)/shard_map/pallas_call | solution.py:259
  64.5 0.6 copy.8
Async XLA Ops:
  0.0 1.6 %copy-start = (bf16[1,8,2,256,256]{4,3,2,1,0:T(8,128)(2,1)S(1)}, bf16[1,8,2,256,256]{4,3,2,1,0:T(8,128)(2,1)}, u32[]{:S(2)}) copy-start(bf16[1,8,2,256,256]{4,3,2,1,0:T(8,128)(2,1)} %elem_hbm.1) | copy-start | bytes 6291460
  1.6 1.4 %copy-start.1 = (bf16[2,3,1,512,256]{4,3,2,1,0:T(8,128)(2,1)S(1)}, bf16[2,3,1,512,256]{4,3,2,1,0:T(8,128)(2,1)}, u32[]{:S(2)}) copy-start(bf16[2,3,1,512,256]{4,3,2,1,0:T(8,128)(2,1)} %vec_hbm.1) | copy-start | bytes 4718596
  3.0 1.1 %copy-start.2 = (bf16[2,3,1,512,128]{4,3,2,1,0:T(8,128)(2,1)S(1)}, bf16[2,3,1,512,128]{4,3,2,1,0:T(8,128)(2,1)}, u32[]{:S(2)}) copy-start(bf16[2,3,1,512,128]{4,3,2,1,0:T(8,128)(2,1)} %prop_hbm.1) | copy-start | bytes 2359300
  4.1 0.7 %copy-start.3 = (s32[1,16]{1,0:T(1,128)S(1)}, s32[1,16]{1,0:T(1,128)}, u32[]{:S(2)}) copy-start(s32[1,16]{1,0:T(1,128)} %sink_hbm.1) | copy-start | bytes 196
  4.8 0.7 %copy-start.4 = (s32[1,16]{1,0:T(1,128)S(1)}, s32[1,16]{1,0:T(1,128)}, u32[]{:S(2)}) copy-start(s32[1,16]{1,0:T(1,128)} %mom_hbm.1) | copy-start | bytes 196

commit v2 on v1

--- a/solution.py
+++ b/solution.py
@@ -16,7 +16,7 @@
 
 def kernel(
     vec_hbm, prop_hbm, elem_hbm, sink_hbm, mom_hbm, out_ref,
-    vec, prop, elem, xsend, xrecv, zsend, zrecv, gath, mix, sink, mom, rows, ranks,
+    vec, prop, elem, xsend, xrecv, zsend, whole, rest_send, zrecv, gath, mix, sink, mom, rows, ranks,
     load_sem, elem_sem, item_sem, item_send, item_recv,
     xs_sem, xr_sem, zs_sem, zr_sem, ys_sem, yr_sem, mix_sem, fs_sem, fr_sem,
 ):
@@ -118,7 +118,11 @@
         pltpu.make_async_copy(xrecv.at[xx], xrecv.at[xx], xr_sem.at[xx]).wait()
         total = total + xrecv[xx]
     for hh in range(2):
-        zsend[hh] = total[:, hh * narrow:(hh + 1) * narrow]
+        part = total[:, hh * narrow:(hh + 1) * narrow]
+        zsend[hh] = part.astype(BF16)
+        whole[hh] = part
+    rest = whole[1 - h]
+    rest_send[0] = (rest - zsend[1 - h].astype(F32)).astype(BF16)
 
     def zcopy(off, slot):
         to = lax.rem(ring + ZR - off, ZR)
@@ -128,6 +132,9 @@
         )
 
     zcopies = [zcopy(off, slot) for slot, off in enumerate(OFFSETS)]
+    zcopies.append(
+        send(rest_send.at[0], zrecv.at[9], zs_sem.at[9], zr_sem.at[9], device(x, y, far, core))
+    )
     for copy in zcopies:
         copy.start()
 
@@ -138,29 +145,64 @@
 
     def arrived(slot):
         pltpu.make_async_copy(zrecv.at[slot], zrecv.at[slot], zr_sem.at[slot]).wait()
-        return zrecv[slot]
-
-    def ysend(src, dst, n, kind, r):
-        yy = lax.rem(y + r, Y)
+        return zrecv[slot].astype(F32)
+
+    sent = []
+
+    def ysend(src, dst, kind, r, origin):
         return send(
-            src, dst, ys_sem.at[kind, r], yr_sem.at[kind, y], device(x, yy, ring, core)
-        )
+            src, dst, ys_sem.at[kind, r], yr_sem.at[kind, origin],
+            device(x, lax.rem(y + r, Y), ring, core),
+        )
+
+    def third(r, slot):
+        return ysend(gath.at[y, slot], gath.at[y, 2], 2, r, y)
+
+    def direct(slot):
+        for r in (2, Y - 2, 1, Y - 1):
+            copy = ysend(gath.at[y, slot], gath.at[y, slot], slot, r, y)
+            copy.start()
+            sent.append(copy)
+
+    def ywait(kind, slot, origin):
+        ref = gath.at[origin, slot]
+        pltpu.make_async_copy(ref, ref, yr_sem.at[kind, origin]).wait()
+
+    below, above = lax.rem(y + Y - 2, Y), lax.rem(y + 2, Y)
+
+    def forward(slot):
+        ywait(slot, slot, above)
+        for r, back in ((Y - 2, 4), (Y - 1, 5)):
+            copy = send(
+                gath.at[above, slot], gath.at[above, slot], ys_sem.at[slot, back],
+                yr_sem.at[slot, above], device(x, lax.rem(y + r, Y), ring, core),
+            )
+            copy.start()
+            sent.append(copy)
+        ywait(slot, slot, below)
+        copy = send(
+            gath.at[below, slot], gath.at[below, slot], ys_sem.at[slot, 3],
+            yr_sem.at[slot, below], device(x, lax.rem(y + 1, Y), ring, core),
+        )
+        copy.start()
+        sent.append(copy)
 
     order = (4, 3, 5, 2, 6, 1, 7)
-    ycopies = []
+    gath[y, 3] = (arrived(6) + arrived(5)).astype(BF16)
+    for r in order:
+        @pl.when(lax.rem(y + r, Y) > y)
+        def _():
+            third(r, 3).start()
+    gath[y, 1] = (arrived(4) + arrived(3)).astype(BF16)
+    direct(1)
     gath[y, 0] = (arrived(2) + arrived(1)).astype(BF16)
-    gath[y, 1] = (arrived(4) + arrived(3)).astype(BF16)
+    direct(0)
+    near = whole[h] + arrived(0)
+    gath[y, 2] = near.astype(BF16)
     for r in order:
-        ycopies.append(ysend(gath.at[y, pl.ds(0, 2)], gath.at[y, pl.ds(0, 2)], 2, 0, r))
-        ycopies[-1].start()
-    gath[y, 3] = (arrived(6) + arrived(5)).astype(BF16)
-    own = (zsend[h] + arrived(0)).astype(BF16)
-    gath[y, 2] = own
-    for r in order:
-        yy = lax.rem(y + r, Y)
-        slot = jnp.where(y >= yy, 2, 3)
-        ycopies.append(ysend(gath.at[y, slot], gath.at[y, 2], 1, 1, r))
-        ycopies[-1].start()
+        @pl.when(lax.rem(y + r, Y) < y)
+        def _():
+            third(r, 2).start()
 
     @pl.when(special)
     def _():
@@ -169,10 +211,13 @@
     slot = jnp.where(special, 4, jnp.where(core == 0, 3, 2))
     step = jnp.where(core == 0, Y - 1, 1)
     extra = send(
-        gath.at[y, slot], gath.at[y, 3], ys_sem.at[2, 0], yr_sem.at[2, 0],
+        gath.at[y, slot], gath.at[y, 3], ys_sem.at[2, 0], yr_sem.at[3, 0],
         device(x, lax.rem(y + step, Y), ring, core),
     )
     extra.start()
+    forward(1)
+    forward(0)
+    own = (near + arrived(9)).astype(BF16)
 
     elem_load.wait()
     stacked = jnp.concatenate([own[0], own[1]], axis=0)
@@ -190,16 +235,17 @@
     mix_copy.wait_recv()
     for r in range(1, Y):
         yy = lax.rem(y + r, Y)
-        both = gath.at[yy, pl.ds(0, 2)]
-        pltpu.make_async_copy(both, both, yr_sem.at[0, yy]).wait()
-        pltpu.make_async_copy(gath.at[yy, 2], gath.at[yy, 2], yr_sem.at[1, yy]).wait()
+        if r not in (2, Y - 2):
+            ywait(0, 0, yy)
+            ywait(1, 1, yy)
+        ywait(2, 2, yy)
     extra.wait_recv()
 
     ranks[...] = jnp.zeros_like(ranks)
     lanes = ranks.shape[-1]
     count = sink.shape[-1]
     for kt in range(2):
-        @pl.loop(0, count)
+        @pl.loop(0, count, unroll=4)
         def _(k):
             rel = sink[kt, k] + (ZL - c) * (2 * Y)
             rel = jnp.where(rel >= ZL * 2 * Y, rel - ZL * 2 * Y, rel)
@@ -243,8 +289,11 @@
     out_ref[0:1] = mine[:, :count]
     out_ref[1:2] = mine[:, count:]
 
-    for copy in xcopies + items + zcopies + ycopies + [extra, mix_copy] + fcopies:
+    for copy in xcopies + items + zcopies + sent + [extra, mix_copy] + fcopies:
         copy.wait_send()
+    for r in order:
+        third(r, 2).wait_send()
+
     @pl.when(special)
     def _():
         zcopy(4 + core, 7).wait_send()
@@ -267,8 +316,10 @@
             pltpu.VMEM((nmom, 2, nvec, nvec), BF16),
             pltpu.VMEM((X, 2, wide, nvec), F32),
             pltpu.VMEM((X, 2, wide, nvec), F32),
+            pltpu.VMEM((2, 2, narrow, nvec), BF16),
             pltpu.VMEM((2, 2, narrow, nvec), F32),
-            pltpu.VMEM((9, 2, narrow, nvec), F32),
+            pltpu.VMEM((1, 2, narrow, nvec), BF16),
+            pltpu.VMEM((10, 2, narrow, nvec), BF16),
             pltpu.VMEM((Y, 5, 2, narrow, nvec), BF16),
             pltpu.VMEM((2, nmom, 2, narrow, nvec), BF16),
             pltpu.SMEM((2, items), jnp.int32),
@@ -276,11 +327,11 @@
             pltpu.VMEM((4 * X, 1, 128), F32),
             pltpu.VMEM((128, 128), F32),
             dma((2, 2, 3)), dma, dma((2,)), dma((2,)), dma((2,)),
-            dma((X,)), dma((X,)), dma((9,)), dma((9,)), dma((3, Y)), dma((3, Y)),
+            dma((X,)), dma((X,)), dma((10,)), dma((10,)), dma((3, Y)), dma((4, Y)),
             dma((2,)), dma((4 * X,)), dma((4 * X,)),
         ],
         compiler_params=pltpu.CompilerParams(
-            collective_id=0, has_side_effects=True, vmem_limit_bytes=32 * 1024 * 1024
+            collective_id=0, has_side_effects=True, vmem_limit_bytes=60 * 1024 * 1024
         ),
     )(eigvecs, propagator, elementals, sink_times, momenta)
     return out[:, None, :]

time: 65.3 us -> 56.1 us (0.86)
  local copies, waits for them, and re-layouts: 6 us -> 1.24 us
  Pallas kernels: 59.1 us -> 54.7 us
    unnamed x11 -> x1, local copies, waits for them, and re-layouts: 6 us -> 1.24 us
    pallas_call x1, Pallas kernels: 59.1 us -> 54.7 us  [on_device(): pl.pallas_call(kernel, out_shape=jax.ShapeDtypeStruct((2, items), F32), i...]
where the time goes in v2:
time: 56.1 us; the launch traced here: 55.9 us
  Pallas kernels  54.7 us (98%)
  local copies, waits for them, and re-layouts  1.24 us (2%)
    pallas_call x1, Pallas kernels, on_device(): pl.pallas_call(kernel, out_shape=jax.ShapeDtypeStruct((2, items), F32), i...  54.7 us
    unnamed x1, local copies, waits for them, and re-layouts  1.24 us

profile of v2, /device:TPU:1, one launch (start us, length us, event | category | flops | bytes accessed | tf_op | source)
XLA Modules:
  0.0 55.9 jit_solution(3482347040385649359)
XLA Ops:
  0.0 54.7 %shard_map.55 = f32[2,16]{1,0:T(2,128)} custom-call(bf16[2,3,1,512,256]{4,3,2,1,0:T(8,128)(2,1)} %vec_hbm.1, bf16[2,3,1,512,128]{4,3,2,1,0:T(8,128)(2,1)} %prop_hbm.1, bf16[1,8,2,256,256]{4,3,2,1,0:T(8,128)(2,1)} %elem_hbm.1, s32[1,16]{1,0:T(1,128)} %sink_hbm.1, s32[1,16]{1,0:T(1,128)} %mom_hbm.1), custom_call_target="tpu_custom_call" | custom-call | tf_op jit(solution)/shard_map/pallas_call | solution.py:308
  54.7 1.2 %copy.8 = f32[2,1,16]{2,1,0:T(1,128)} copy(f32[2,1,16]{2,1,0:T(1,128)} %bitcast.3) | data formatting | bytes 256

commit v3 on v2

--- a/solution.py
+++ b/solution.py
@@ -17,7 +17,7 @@
 def kernel(
     vec_hbm, prop_hbm, elem_hbm, sink_hbm, mom_hbm, out_ref,
     vec, prop, elem, xsend, xrecv, zsend, whole, rest_send, zrecv, gath, mix, sink, mom, rows, ranks,
-    load_sem, elem_sem, item_sem, item_send, item_recv,
+    near_sem, load_sem, elem_sem, item_sem, item_send, item_recv,
     xs_sem, xr_sem, zs_sem, zr_sem, ys_sem, yr_sem, mix_sem, fs_sem, fr_sem,
 ):
     tm, space = lax.axis_index("tm"), lax.axis_index("space")
@@ -70,11 +70,21 @@
         copy.start()
 
     barrier = pltpu.get_barrier_semaphore()
-    partners = [final_device(*d) for d in final]
-    partners += [device(x, lax.rem(y + r, Y), ring, core) for r in range(1, Y)]
-    partners += [device(x, y, lax.rem(ring + r, ZR), core) for r in range(1, ZR) if r != ZL]
-    for where in partners:
-        pl.semaphore_signal(barrier, inc=1, device_id=where, device_id_type=pl.DeviceIdType.MESH)
+    other = device(x, y, ring, 1 - core)
+
+    def along_y(r):
+        return device(x, lax.rem(y + r + Y, Y), ring, core)
+
+    def along_z(r):
+        return device(x, y, lax.rem(ring + r + ZR, ZR), core)
+
+    def tell(sem, devices):
+        for where in devices:
+            pl.semaphore_signal(sem, inc=1, device_id=where, device_id_type=pl.DeviceIdType.MESH)
+
+    partners = [device(lax.rem(x + d, X), y, ring, core) for d in range(1, X)] + [other]
+    partners += [along_y(1), along_y(-1), along_z(1), along_z(-1)]
+    tell(barrier, partners)
 
     dims = (((0,), (0,)), ((), ()))
     real = imag = None
@@ -103,7 +113,8 @@
         )
         copy.start()
         xcopies.append(copy)
-    other = device(x, y, ring, 1 - core)
+    tell(near_sem.at[0], [along_z(1), along_z(-1)])
+    tell(near_sem.at[1], [along_y(1), along_y(-1)])
     for copy in own_items:
         copy.wait()
     items = [
@@ -112,6 +123,12 @@
     ]
     for copy in items:
         copy.start()
+    pl.semaphore_wait(near_sem.at[0], 2)
+    tell(near_sem.at[2], [along_z(2), along_z(-2)])
+    pl.semaphore_wait(near_sem.at[1], 2)
+    tell(near_sem.at[3], [along_y(2), along_y(-2)])
+    pl.semaphore_wait(near_sem.at[2], 2)
+    tell(near_sem.at[4], [along_z(2), along_z(-2)])
     total = xsend[x]
     for d in (1, 3, 2):
         xx = lax.rem(x + d, X)
@@ -135,6 +152,7 @@
     zcopies.append(
         send(rest_send.at[0], zrecv.at[9], zs_sem.at[9], zr_sem.at[9], device(x, y, far, core))
     )
+    pl.semaphore_wait(near_sem.at[4], 2)
     for copy in zcopies:
         copy.start()
 
@@ -189,6 +207,7 @@
 
     order = (4, 3, 5, 2, 6, 1, 7)
     gath[y, 3] = (arrived(6) + arrived(5)).astype(BF16)
+    pl.semaphore_wait(near_sem.at[3], 2)
     for r in order:
         @pl.when(lax.rem(y + r, Y) > y)
         def _():
@@ -326,7 +345,7 @@
             pltpu.SMEM((2, items), jnp.int32),
             pltpu.VMEM((4 * X, 1, 128), F32),
             pltpu.VMEM((128, 128), F32),
-            dma((2, 2, 3)), dma, dma((2,)), dma((2,)), dma((2,)),
+            pltpu.SemaphoreType.REGULAR((5,)), dma((2, 2, 3)), dma, dma((2,)), dma((2,)), dma((2,)),
             dma((X,)), dma((X,)), dma((10,)), dma((10,)), dma((3, Y)), dma((4, Y)),
             dma((2,)), dma((4 * X,)), dma((4 * X,)),
         ],

time: 56.1 us -> 50.1 us (0.89)
  Pallas kernels: 54.7 us -> 48.7 us
    pallas_call x1, Pallas kernels: 54.7 us -> 48.7 us  [on_device(): pl.pallas_call(kernel, out_shape=jax.ShapeDtypeStruct((2, items), F32), i...]
where the time goes in v3:
time: 50.1 us; the launch traced here: 50 us
  Pallas kernels  48.7 us (97%)
  local copies, waits for them, and re-layouts  1.24 us (2%)
    pallas_call x1, Pallas kernels, on_device(): pl.pallas_call(kernel, out_shape=jax.ShapeDtypeStruct((2, items), F32), i...  48.7 us
    unnamed x1, local copies, waits for them, and re-layouts  1.24 us

profile of v3, /device:TPU:1, one launch (start us, length us, event | category | flops | bytes accessed | tf_op | source)
XLA Modules:
  0.0 50.0 jit_solution(12927021951140433770)
XLA Ops:
  0.0 48.7 %shard_map.55 = f32[2,16]{1,0:T(2,128)} custom-call(bf16[2,3,1,512,256]{4,3,2,1,0:T(8,128)(2,1)} %vec_hbm.1, bf16[2,3,1,512,128]{4,3,2,1,0:T(8,128)(2,1)} %prop_hbm.1, bf16[1,8,2,256,256]{4,3,2,1,0:T(8,128)(2,1)} %elem_hbm.1, s32[1,16]{1,0:T(1,128)} %sink_hbm.1, s32[1,16]{1,0:T(1,128)} %mom_hbm.1), custom_call_target="tpu_custom_call" | custom-call | tf_op jit(solution)/shard_map/pallas_call | solution.py:327
  48.7 1.2 %copy.8 = f32[2,1,16]{2,1,0:T(1,128)} copy(f32[2,1,16]{2,1,0:T(1,128)} %bitcast.3) | data formatting | bytes 256

commit v4 on v3

--- a/solution.py
+++ b/solution.py
@@ -92,6 +92,10 @@
         for q in range(2):
             for copy in loads[q * 3 + col]:
                 copy.wait()
+        if col == 2:
+            pl.semaphore_wait(barrier, len(partners))
+            tell(near_sem.at[0], [along_z(1), along_z(-1)])
+            tell(near_sem.at[1], [along_y(1), along_y(-1)])
         vr, vi = vec[0, col], vec[1, col]
         pr, pi = prop[0, col], prop[1, col]
         dot = functools.partial(lax.dot_general, dimension_numbers=dims, preferred_element_type=F32)
@@ -100,21 +104,22 @@
         real = re if real is None else real + re
         imag = im if imag is None else imag + im
     for xx in range(X):
-        xsend[xx, 0] = real[xx * wide:(xx + 1) * wide]
-        xsend[xx, 1] = imag[xx * wide:(xx + 1) * wide]
-
-    pl.semaphore_wait(barrier, len(partners))
+        for hh in range(2):
+            first = xx * wide + hh * narrow
+            xsend[hh, xx, 0] = real[first:first + narrow]
+            xsend[hh, xx, 1] = imag[first:first + narrow]
+
 
     xcopies = []
-    for d in (2, 1, 3):
-        xx = lax.rem(x + d, X)
-        copy = send(
-            xsend.at[xx], xrecv.at[x], xs_sem.at[d], xr_sem.at[x], device(xx, y, ring, core)
-        )
-        copy.start()
-        xcopies.append(copy)
-    tell(near_sem.at[0], [along_z(1), along_z(-1)])
-    tell(near_sem.at[1], [along_y(1), along_y(-1)])
+    for turn, hh in enumerate((h, 1 - h)):
+        for d in (2, 1, 3):
+            xx = lax.rem(x + d, X)
+            copy = send(
+                xsend.at[hh, xx], xrecv.at[hh, x], xs_sem.at[turn, d], xr_sem.at[turn, x],
+                device(xx, y, ring, core),
+            )
+            copy.start()
+            xcopies.append(copy)
     for copy in own_items:
         copy.wait()
     items = [
@@ -124,22 +129,21 @@
     for copy in items:
         copy.start()
     pl.semaphore_wait(near_sem.at[0], 2)
-    tell(near_sem.at[2], [along_z(2), along_z(-2)])
+    tell(near_sem.at[2], [along_z(-2)])
+    tell(near_sem.at[6], [along_z(2)])
     pl.semaphore_wait(near_sem.at[1], 2)
     tell(near_sem.at[3], [along_y(2), along_y(-2)])
-    pl.semaphore_wait(near_sem.at[2], 2)
-    tell(near_sem.at[4], [along_z(2), along_z(-2)])
-    total = xsend[x]
-    for d in (1, 3, 2):
-        xx = lax.rem(x + d, X)
-        pltpu.make_async_copy(xrecv.at[xx], xrecv.at[xx], xr_sem.at[xx]).wait()
-        total = total + xrecv[xx]
-    for hh in range(2):
-        part = total[:, hh * narrow:(hh + 1) * narrow]
-        zsend[hh] = part.astype(BF16)
-        whole[hh] = part
-    rest = whole[1 - h]
-    rest_send[0] = (rest - zsend[1 - h].astype(F32)).astype(BF16)
+    pl.semaphore_wait(near_sem.at[2], 1)
+    tell(near_sem.at[4], [along_z(-2)])
+    def summed(turn, hh):
+        total = xsend[hh, x]
+        for d in (1, 3, 2):
+            xx = lax.rem(x + d, X)
+            ref = xrecv.at[hh, xx]
+            pltpu.make_async_copy(ref, ref, xr_sem.at[turn, xx]).wait()
+            total = total + xrecv[hh, xx]
+        zsend[hh] = total.astype(BF16)
+        return total
 
     def zcopy(off, slot):
         to = lax.rem(ring + ZR - off, ZR)
@@ -152,12 +156,45 @@
     zcopies.append(
         send(rest_send.at[0], zrecv.at[9], zs_sem.at[9], zr_sem.at[9], device(x, y, far, core))
     )
-    pl.semaphore_wait(near_sem.at[4], 2)
-    for copy in zcopies:
-        copy.start()
+    def same_half(off):
+        return lax.div(lax.rem(ring + ZR - off, ZR), ZL) == h
+
+    early = ring < 3
+
+    @pl.when(jnp.logical_not(early))
+    def _():
+        pl.semaphore_wait(near_sem.at[6], 1)
+
+    whole[0] = summed(0, h)
+    for n in (6, 4, 2, 3, 5):
+        @pl.when(same_half(OFFSETS[n]))
+        def _():
+            zcopies[n].start()
+
+    rest = summed(1, 1 - h)
+    rest_send[0] = (rest - zsend[1 - h].astype(F32)).astype(BF16)
+    for n in (3, 5, 4, 2):
+        @pl.when(jnp.logical_not(same_half(OFFSETS[n])))
+        def _():
+            zcopies[n].start()
+
+    @pl.when(jnp.logical_not(jnp.logical_or(same_half(OFFSETS[6]), early)))
+    def _():
+        zcopies[6].start()
+
+    pl.semaphore_wait(near_sem.at[4], 1)
+    for n in (0, 1, 7):
+        zcopies[n].start()
+
+    @pl.when(early)
+    def _():
+        pl.semaphore_wait(near_sem.at[6], 1)
+        zcopies[6].start()
 
     @pl.when(special)
     def _():
+        tell(near_sem.at[5], [along_z(2)])
+        pl.semaphore_wait(near_sem.at[5], 1)
         zcopy(4 + core, 7).start()
         zcopy(10 + core, 8).start()
 
@@ -190,7 +227,7 @@
 
     def forward(slot):
         ywait(slot, slot, above)
-        for r, back in ((Y - 2, 4), (Y - 1, 5)):
+        for r, back in ((Y - 2, 4), (Y - 1, 5))[slot:]:
             copy = send(
                 gath.at[above, slot], gath.at[above, slot], ys_sem.at[slot, back],
                 yr_sem.at[slot, above], device(x, lax.rem(y + r, Y), ring, core),
@@ -198,12 +235,13 @@
             copy.start()
             sent.append(copy)
         ywait(slot, slot, below)
-        copy = send(
-            gath.at[below, slot], gath.at[below, slot], ys_sem.at[slot, 3],
-            yr_sem.at[slot, below], device(x, lax.rem(y + 1, Y), ring, core),
-        )
-        copy.start()
-        sent.append(copy)
+        for r, back in ((2, 4), (1, 3))[1 - slot:]:
+            copy = send(
+                gath.at[below, slot], gath.at[below, slot], ys_sem.at[slot, back],
+                yr_sem.at[slot, below], device(x, lax.rem(y + r, Y), ring, core),
+            )
+            copy.start()
+            sent.append(copy)
 
     order = (4, 3, 5, 2, 6, 1, 7)
     gath[y, 3] = (arrived(6) + arrived(5)).astype(BF16)
@@ -216,7 +254,7 @@
     direct(1)
     gath[y, 0] = (arrived(2) + arrived(1)).astype(BF16)
     direct(0)
-    near = whole[h] + arrived(0)
+    near = whole[0] + arrived(0)
     gath[y, 2] = near.astype(BF16)
     for r in order:
         @pl.when(lax.rem(y + r, Y) < y)
@@ -264,7 +302,7 @@
     lanes = ranks.shape[-1]
     count = sink.shape[-1]
     for kt in range(2):
-        @pl.loop(0, count, unroll=4)
+        @pl.loop(0, count, unroll=16)
         def _(k):
             rel = sink[kt, k] + (ZL - c) * (2 * Y)
             rel = jnp.where(rel >= ZL * 2 * Y, rel - ZL * 2 * Y, rel)
@@ -322,7 +360,7 @@
 def on_device(eigvecs, propagator, elementals, sink_times, momenta):
     nvec, cols, sites = eigvecs.shape[-1], propagator.shape[-1], eigvecs.shape[3]
     nmom, items = elementals.shape[1], sink_times.shape[1]
-    wide, narrow = cols // X, cols // X // 2
+    narrow = cols // X // 2
     dma = pltpu.SemaphoreType.DMA
     out = pl.pallas_call(
         kernel,
@@ -333,10 +371,10 @@
             pltpu.VMEM((2, 3, sites, nvec), BF16),
             pltpu.VMEM((2, 3, sites, cols), BF16),
             pltpu.VMEM((nmom, 2, nvec, nvec), BF16),
-            pltpu.VMEM((X, 2, wide, nvec), F32),
-            pltpu.VMEM((X, 2, wide, nvec), F32),
+            pltpu.VMEM((2, X, 2, narrow, nvec), F32),
+            pltpu.VMEM((2, X, 2, narrow, nvec), F32),
             pltpu.VMEM((2, 2, narrow, nvec), BF16),
-            pltpu.VMEM((2, 2, narrow, nvec), F32),
+            pltpu.VMEM((1, 2, narrow, nvec), F32),
             pltpu.VMEM((1, 2, narrow, nvec), BF16),
             pltpu.VMEM((10, 2, narrow, nvec), BF16),
             pltpu.VMEM((Y, 5, 2, narrow, nvec), BF16),
@@ -345,8 +383,8 @@
             pltpu.SMEM((2, items), jnp.int32),
             pltpu.VMEM((4 * X, 1, 128), F32),
             pltpu.VMEM((128, 128), F32),
-            pltpu.SemaphoreType.REGULAR((5,)), dma((2, 2, 3)), dma, dma((2,)), dma((2,)), dma((2,)),
-            dma((X,)), dma((X,)), dma((10,)), dma((10,)), dma((3, Y)), dma((4, Y)),
+            pltpu.SemaphoreType.REGULAR((7,)), dma((2, 2, 3)), dma, dma((2,)), dma((2,)), dma((2,)),
+            dma((2, X)), dma((2, X)), dma((10,)), dma((10,)), dma((3, Y)), dma((4, Y)),
             dma((2,)), dma((4 * X,)), dma((4 * X,)),
         ],
         compiler_params=pltpu.CompilerParams(

time: 50.1 us -> 47.3 us (0.944)
  Pallas kernels: 48.7 us -> 45.9 us
    pallas_call x1, Pallas kernels: 48.7 us -> 45.9 us  [on_device(): pl.pallas_call(kernel, out_shape=jax.ShapeDtypeStruct((2, items), F32), i...]
where the time goes in v4:
time: 47.3 us; the launch traced here: 47.2 us
  Pallas kernels  45.9 us (97%)
  local copies, waits for them, and re-layouts  1.24 us (3%)
    pallas_call x1, Pallas kernels, on_device(): pl.pallas_call(kernel, out_shape=jax.ShapeDtypeStruct((2, items), F32), i...  45.9 us
    unnamed x1, local copies, waits for them, and re-layouts  1.24 us

profile of v4, /device:TPU:1, one launch (start us, length us, event | category | flops | bytes accessed | tf_op | source)
XLA Modules:
  0.0 47.2 jit_solution(9918559330516590314)
XLA Ops:
  0.0 45.9 %shard_map.55 = f32[2,16]{1,0:T(2,128)} custom-call(bf16[2,3,1,512,256]{4,3,2,1,0:T(8,128)(2,1)} %vec_hbm.1, bf16[2,3,1,512,128]{4,3,2,1,0:T(8,128)(2,1)} %prop_hbm.1, bf16[1,8,2,256,256]{4,3,2,1,0:T(8,128)(2,1)} %elem_hbm.1, s32[1,16]{1,0:T(1,128)} %sink_hbm.1, s32[1,16]{1,0:T(1,128)} %mom_hbm.1), custom_call_target="tpu_custom_call" | custom-call | tf_op jit(solution)/shard_map/pallas_call | solution.py:365
  45.9 1.2 %copy.8 = f32[2,1,16]{2,1,0:T(1,128)} copy(f32[2,1,16]{2,1,0:T(1,128)} %bitcast.3) | data formatting | bytes 256

commit v5 on v4

--- a/solution.py
+++ b/solution.py
@@ -244,23 +244,22 @@
             sent.append(copy)
 
     order = (4, 3, 5, 2, 6, 1, 7)
+    pl.semaphore_wait(near_sem.at[3], 2)
+    gath[y, 1] = (arrived(4) + arrived(3)).astype(BF16)
+    direct(1)
+    gath[y, 0] = (arrived(2) + arrived(1)).astype(BF16)
+    direct(0)
     gath[y, 3] = (arrived(6) + arrived(5)).astype(BF16)
-    pl.semaphore_wait(near_sem.at[3], 2)
     for r in order:
         @pl.when(lax.rem(y + r, Y) > y)
         def _():
             third(r, 3).start()
-    gath[y, 1] = (arrived(4) + arrived(3)).astype(BF16)
-    direct(1)
-    gath[y, 0] = (arrived(2) + arrived(1)).astype(BF16)
-    direct(0)
     near = whole[0] + arrived(0)
     gath[y, 2] = near.astype(BF16)
     for r in order:
         @pl.when(lax.rem(y + r, Y) < y)
         def _():
             third(r, 2).start()
-
     @pl.when(special)
     def _():
         gath[y, 4] = (arrived(7) + arrived(8)).astype(BF16)

time: 47.3 us -> 46 us (0.973)
  Pallas kernels: 45.9 us -> 44.6 us
    pallas_call x1, Pallas kernels: 45.9 us -> 44.6 us  [on_device(): pl.pallas_call(kernel, out_shape=jax.ShapeDtypeStruct((2, items), F32), i...]
where the time goes in v5:
time: 46 us; the launch traced here: 45.9 us
  Pallas kernels  44.6 us (97%)
  local copies, waits for them, and re-layouts  1.24 us (3%)
    pallas_call x1, Pallas kernels, on_device(): pl.pallas_call(kernel, out_shape=jax.ShapeDtypeStruct((2, items), F32), i...  44.6 us
    unnamed x1, local copies, waits for them, and re-layouts  1.24 us

profile of v5, /device:TPU:1, one launch (start us, length us, event | category | flops | bytes accessed | tf_op | source)
XLA Modules:
  0.0 45.9 jit_solution(1639312876356585879)
XLA Ops:
  0.0 44.6 %shard_map.55 = f32[2,16]{1,0:T(2,128)} custom-call(bf16[2,3,1,512,256]{4,3,2,1,0:T(8,128)(2,1)} %vec_hbm.1, bf16[2,3,1,512,128]{4,3,2,1,0:T(8,128)(2,1)} %prop_hbm.1, bf16[1,8,2,256,256]{4,3,2,1,0:T(8,128)(2,1)} %elem_hbm.1, s32[1,16]{1,0:T(1,128)} %sink_hbm.1, s32[1,16]{1,0:T(1,128)} %mom_hbm.1), custom_call_target="tpu_custom_call" | custom-call | tf_op jit(solution)/shard_map/pallas_call | solution.py:364
  44.6 1.2 %copy.8 = f32[2,1,16]{2,1,0:T(1,128)} copy(f32[2,1,16]{2,1,0:T(1,128)} %bitcast.3) | data formatting | bytes 256

commit v6 on v5

--- a/solution.py
+++ b/solution.py
@@ -44,7 +44,7 @@
         jnp.logical_and(y == 0, core == 0), jnp.logical_and(y == Y - 1, core == 1)
     )
     final = [
-        (dx, dz, dk) for dz in range(2) for dx in range(X) for dk in range(2) if dx or dz or dk
+        (dx, dz, dk) for dz in (1, 0) for dx in (2, 1, 3, 0) for dk in range(2) if dx or dz or dk
     ]
 
     def final_device(dx, dz, dk):
@@ -243,7 +243,7 @@
             copy.start()
             sent.append(copy)
 
-    order = (4, 3, 5, 2, 6, 1, 7)
+    order = (1, 7, 2, 6, 3, 5, 4)
     pl.semaphore_wait(near_sem.at[3], 2)
     gath[y, 1] = (arrived(4) + arrived(3)).astype(BF16)
     direct(1)

time: 46 us -> 45.7 us (level)
  no operation moved by 1% of the time
where the time goes in v6:
time: 45.7 us; the launch traced here: 45.5 us
  Pallas kernels  44.3 us (97%)
  local copies, waits for them, and re-layouts  1.24 us (3%)
    pallas_call x1, Pallas kernels, on_device(): pl.pallas_call(kernel, out_shape=jax.ShapeDtypeStruct((2, items), F32), i...  44.3 us
    unnamed x1, local copies, waits for them, and re-layouts  1.24 us

profile of v6, /device:TPU:1, one launch (start us, length us, event | category | flops | bytes accessed | tf_op | source)
XLA Modules:
  0.0 45.5 jit_solution(4993754803207931961)
XLA Ops:
  0.0 44.3 %shard_map.55 = f32[2,16]{1,0:T(2,128)} custom-call(bf16[2,3,1,512,256]{4,3,2,1,0:T(8,128)(2,1)} %vec_hbm.1, bf16[2,3,1,512,128]{4,3,2,1,0:T(8,128)(2,1)} %prop_hbm.1, bf16[1,8,2,256,256]{4,3,2,1,0:T(8,128)(2,1)} %elem_hbm.1, s32[1,16]{1,0:T(1,128)} %sink_hbm.1, s32[1,16]{1,0:T(1,128)} %mom_hbm.1), custom_call_target="tpu_custom_call" | custom-call | tf_op jit(solution)/shard_map/pallas_call | solution.py:364
  44.3 1.2 %copy.8 = f32[2,1,16]{2,1,0:T(1,128)} copy(f32[2,1,16]{2,1,0:T(1,128)} %bitcast.3) | data formatting | bytes 256
